TPU v7x, 32 devices: a whole 2x2x4 slice. The times are simulated.
32 devices in a mesh: cam: 16 (over z, y, core), frame: 2 (over x).
Axes of the slice: x: 2, y: 2, z: 4, core: 2. Of those that a mesh axis runs over, the one named last changes fastest.
Arguments:
- frames: bfloat16 [16, 64, 3, 4096], P('cam', 'frame'), may hold values from -6 to 6
- conv1_w: bfloat16 [27, 128], replicated, may hold values from -1.25 to 1.25
- conv2_w: bfloat16 [1152, 256], replicated, may hold values from -0.1875 to 0.1875
- tile_w: bfloat16 [256, 128], replicated, may hold values from -0.375 to 0.375
- vis_subject: int32 [16, 64, 12], P('cam', 'frame'), may hold values from 0 to 63, as said below
- part_count: int32 [16, 64, 12], P('cam', 'frame'), may hold values from 6 to 8
- part_region: int32 [16, 64, 12, 8], P('cam', 'frame'), may hold values from 0 to 15
- subject_slot: int32 [64], replicated, may hold values from 0 to 63, as said below
- qkv_w: bfloat16 [1024, 3072], replicated, may hold values from -0.1875 to 0.1875
- out_w: bfloat16 [1024, 1024], replicated, may hold values from -0.1875 to 0.1875
- key_bias: float32 [64, 16, 64], P('cam'), may hold values from -2 to 237
Outputs:
- posed: bfloat16 [64, 64, 1024], P('cam', 'frame')
Inputs may be any that keep to these rules, and one draw needn't show every extreme that they name: `vis_subject`: each camera frame lists 12 distinct subjects. Rows of the subject-owned arrays form blocks of 4 (the rows of one index of cam); one list names at most 2 subjects whose rows lie in one block, and for each aligned block of 32 frames one row block, drawn for it, has exactly 2 subjects in every camera's list of every frame of it. `subject_slot`: A permutation of the subjects' numbers.
All inputs are finite; a program needn't handle non-finite values.
Results may differ from a plain program's by a relative error of at most 0.0085.
Values may be sent and summed in bfloat16 or wider, within the bound.
No kernel may reach another device: no remote copies, remote signals or barrier semaphores. Data moves between devices by JAX's collectives and lax.ppermute only.
A program may use at most 64 MiB of HBM per device.

v0:
```python
import math
import jax
import jax.numpy as jnp
from jax import lax
from jax.sharding import PartitionSpec as P

IMG = 64
RGRID = 4
C1 = 128
C2 = 256
TILE = 128
HEADS = 16
SUBJ_DEV = 4
PER_OWN = 2
EPS = 1e-05
NEG_START = -1e30


def conv_features(pictures, conv1_w, conv2_w):
    amount = pictures.shape[0]
    images = pictures.reshape(amount, 3, IMG, IMG)
    section_one = lax.conv_general_dilated(
        images,
        conv1_w.reshape(3, 3, 3, C1),
        (2, 2),
        ((1, 1), (1, 1)),
        dimension_numbers=("NCHW", "HWIO", "NHWC"),
        preferred_element_type=jnp.float32,
    )
    section_one = jax.nn.relu(section_one).astype(jnp.bfloat16)
    section_two = lax.conv_general_dilated(
        section_one,
        conv2_w.reshape(3, 3, C1, C2),
        (2, 2),
        ((1, 1), (1, 1)),
        dimension_numbers=("NHWC", "HWIO", "NHWC"),
        preferred_element_type=jnp.float32,
    )
    section_two = jax.nn.relu(section_two)
    patch_side = IMG // (4 * RGRID)
    pooled = jnp.mean(
        section_two.reshape(amount, RGRID, patch_side, RGRID, patch_side, C2), axis=(2, 4)
    )
    return pooled.reshape(amount, RGRID * RGRID, C2).astype(jnp.bfloat16)


def select_parts(features, part_region, part_count):
    frames_here, listed, part_total = part_region.shape
    regions = features.shape[1]
    visible = jnp.arange(part_total, dtype=jnp.int32)[None, None, :] < part_count[:, :, None]
    chooser = (part_region[:, :, :, None] == jnp.arange(regions, dtype=jnp.int32)) & visible[
        :, :, :, None
    ]
    chooser = chooser.astype(jnp.bfloat16).reshape(frames_here, listed * part_total, regions)
    picked = jnp.einsum("fer,frc->fec", chooser, features, preferred_element_type=jnp.float32)
    return picked.astype(jnp.bfloat16).reshape(frames_here * listed, part_total * features.shape[2])


def build_buffers(payload, vis_subject, subject_slot, owners, frames_here):
    listed = vis_subject.shape[1]
    entries = frames_here * listed
    subjects = subject_slot.shape[0]
    flat_ids = vis_subject.reshape(entries)
    slot_rows = jnp.sum(
        jnp.where(
            flat_ids[:, None] == jnp.arange(subjects, dtype=jnp.int32), subject_slot[None, :], 0
        ),
        axis=1,
    )
    owner_index = slot_rows // SUBJ_DEV
    member = (owner_index[:, None] == jnp.arange(owners, dtype=jnp.int32)).astype(jnp.int32)
    arrival = jnp.sum((jnp.cumsum(member, axis=0) - 1) * member, axis=1)
    capacity = PER_OWN * frames_here
    target = owner_index * capacity + arrival
    source = (
        jnp.full((owners * capacity,), entries, jnp.int32)
        .at[target]
        .set(jnp.arange(entries, dtype=jnp.int32))
    )
    padded = jnp.concatenate([payload, jnp.zeros((1, payload.shape[1]), payload.dtype)], axis=0)
    frame_of = jnp.arange(entries, dtype=jnp.int32) // listed
    placement_code = slot_rows % SUBJ_DEV * frames_here + frame_of
    codes = jnp.concatenate([placement_code, jnp.full((1,), SUBJ_DEV * frames_here, jnp.int32)])
    outgoing = padded[source].reshape(owners, capacity, payload.shape[1])
    return (outgoing, codes[source].reshape(owners, capacity))


def collect_tokens(received, arrived, rows):
    flat_rows = received.reshape(-1, received.shape[2])
    picker = (jnp.arange(rows, dtype=jnp.int32)[:, None] == arrived.reshape(1, -1)).astype(
        jnp.bfloat16
    )
    return jnp.dot(picker, flat_rows, preferred_element_type=jnp.float32)


def per_device(
    frames,
    conv1_w,
    conv2_w,
    tile_w,
    vis_subject,
    part_count,
    part_region,
    subject_slot,
    qkv_w,
    out_w,
    key_bias,
):
    pictures = frames[0]
    frames_here = pictures.shape[0]
    owners = lax.axis_size("cam")
    pooled = conv_features(pictures, conv1_w, conv2_w)
    projected = jnp.dot(pooled.reshape(-1, C2), tile_w, preferred_element_type=jnp.float32)
    tiles = projected.astype(jnp.bfloat16).reshape(frames_here, -1, TILE)
    payload = select_parts(tiles, part_region[0], part_count[0])
    outgoing, codes = build_buffers(payload, vis_subject[0], subject_slot, owners, frames_here)
    received, arrived = (
        lax.all_to_all(outgoing, "cam", split_axis=0, concat_axis=0, tiled=True),
        lax.all_to_all(codes, "cam", split_axis=0, concat_axis=0, tiled=True),
    )
    tokens = collect_tokens(received, arrived, SUBJ_DEV * frames_here)
    width = tokens.shape[1]
    head_size = width // HEADS
    score_scale = 1.0 / math.sqrt(head_size)
    normed = (tokens * lax.rsqrt(jnp.mean(tokens * tokens, axis=1, keepdims=True) + EPS)).astype(
        jnp.bfloat16
    )
    mixed = jnp.dot(normed, qkv_w, preferred_element_type=jnp.float32).astype(jnp.bfloat16)
    queries = mixed[:, :width].reshape(SUBJ_DEV, frames_here, HEADS, head_size)
    key_rows = mixed[:, width : 2 * width].reshape(SUBJ_DEV, frames_here, width)
    value_rows = mixed[:, 2 * width :].reshape(SUBJ_DEV, frames_here, width)
    row_top = jnp.full((SUBJ_DEV, HEADS, frames_here), NEG_START, jnp.float32)
    key_piece = lax.all_gather(key_rows, "frame", axis=1, tiled=True)
    value_piece = lax.all_gather(value_rows, "frame", axis=1, tiled=True)
    span = key_piece.shape[1]
    scores = (
        jnp.einsum(
            "sqhd,skhd->shqk",
            queries,
            key_piece.reshape(SUBJ_DEV, span, HEADS, head_size),
            preferred_element_type=jnp.float32,
        )
        * score_scale
    )
    scores = scores + key_bias[:, :, None, :]
    new_top = jnp.maximum(row_top, jnp.max(scores, axis=3))
    weights = jnp.exp(scores - new_top[..., None])
    denominator = jnp.sum(weights, axis=3)
    numerator = jnp.einsum(
        "shqk,skhd->shqd",
        weights.astype(jnp.bfloat16),
        value_piece.reshape(SUBJ_DEV, span, HEADS, head_size),
        preferred_element_type=jnp.float32,
    )
    row_top, denominator, numerator = (new_top, denominator, numerator)
    attended = numerator / denominator[..., None]
    attended = (
        jnp.transpose(attended, (0, 2, 1, 3))
        .reshape(SUBJ_DEV * frames_here, width)
        .astype(jnp.bfloat16)
    )
    posed = tokens + jnp.dot(attended, out_w, preferred_element_type=jnp.float32)
    return posed.astype(jnp.bfloat16).reshape(SUBJ_DEV, frames_here, width)


def solution(mesh):
    in_specs = (
        P("cam", "frame", None, None),
        P(),
        P(),
        P(),
        P("cam", "frame", None),
        P("cam", "frame", None),
        P("cam", "frame", None, None),
        P(),
        P(),
        P(),
        P("cam", None, None),
    )
    out_specs = P("cam", "frame", None)
    return jax.shard_map(
        per_device, mesh=mesh, in_specs=in_specs, out_specs=out_specs, check_vma=False
    )
```

profile of v0, /device:TPU:12, one launch (start us, length us, event | category | flops | bytes accessed | tf_op | source)
XLA Modules:
  0.0 141.6 jit_solution(5429485537469918314)
XLA Ops:
  0.0 0.9 copy.44
  1.0 0.8 select_reduce_fusion
  1.8 0.9 reduce-window.6
  3.1 2.9 %scatter_custom_fusion = s32[1024]{0:T(1024)S(1)} fusion(s32[384]{0:T(512)S(1)} %fusion.35, s32[384]{0:T(512)S(1)} %iota.33, s32[]{:T(128)} %constant.64.clone.1), kind=kCustom, calls=%fused_computation.78 | custom fusion | bytes 4100 | tf_op jit(solution)/shard_map/scatter | solution.py:78
  6.1 6.9 %gather_fusion = s32[1024]{0:T(1024)S(1)} fusion(s32[385]{0:T(512)S(1)} %pad_add_fusion, s32[1024]{0:T(1024)S(1)} %fusion.23), kind=kCustom, calls=%fused_computation | custom fusion | bytes 12288 | tf_op jit(solution)/shard_map/gather | solution.py:85
  13.0 0.7 all_to_all.9
  13.6 6.2 %all-to-all-start = ((s32[16,1,64]{2,1,0:T(1,128)}), s32[16,1,64]{2,1,0:T(1,128)S(1)}, u32[]{:S(2)}, u32[]{:S(2)}) async-start(s32[16,1,64]{2,1,0:T(1,128)} %all_to_all.9), calls=%async_computation | async-start | bytes 16384 | tf_op jit(solution)/shard_map/all_to_all | solution.py:119
  19.9 4.7 %copy.54 = bf16[1,32,3,4096]{1,2,3,0:T(4,128)(2,1)} copy(bf16[1,32,3,4096]{3,1,2,0:T(8,128)(2,1)S(1)} %copy-done.1) | data formatting | bytes 1572864 | tf_op jit(solution)/shard_map/reshape;squeeze | solution.py:21
  24.6 15.4 %broadcast_maximum_fusion = f32[32,16,16,256]{3,0,2,1:T(8,128)} fusion(bf16[3,3,128,256]{3,2,1,0:T(8,128)(2,1)S(1)} %bitcast.76, bf16[32,3,64,64]{0,1,3,2:T(4,128)(2,1)} %bitcast.68, bf16[3,3,3,128]{3,2,1,0:T(4,128)(2,1)S(1)} %reshape.171), kind=kOutput, calls=%fused_computation.6 | convolution fusion | flops 4864892928 | bytes 9771776 | tf_op jit(solution)/shard_map/conv_general_dilated | solution.py:31
  40.0 4.4 %reduce_sum.56 = f32[32,4,4,256]{3,0,2,1:T(8,128)S(1)} reduce(f32[32,4,4,4,4,256]{5,0,4,3,2,1:T(8,128)} %bitcast.67, f32[]{:T(128)} %constant.69.clone.1), dimensions={2,4}, to_apply=%region_5.6 | reduce | flops 1966080 | bytes 8912900 | tf_op jit(solution)/shard_map/reduce_sum | solution.py:41
  45.1 0.2 convolution_convert_fusion.2
  45.4 0.6 convolution_convert_fusion.1
  46.0 1.2 reshape.175
  47.2 1.2 concatenate.7
  48.4 5.4 %gather_fusion.1 = bf16[1024,1024]{1,0:T(8,128)(2,1)} fusion(bf16[385,1024]{1,0:T(8,128)(2,1)S(1)} %concatenate.7, s32[1024]{0:T(1024)S(1)} %fusion.23), kind=kCustom, calls=%fused_computation.1 | custom fusion | bytes 4198400 | tf_op jit(solution)/shard_map/gather | solution.py:84
  53.8 6.0 %all-to-all-start.1 = ((bf16[16,64,1024]{2,1,0:T(8,128)(2,1)}), bf16[16,64,1024]{2,1,0:T(8,128)(2,1)}, u32[]{:S(2)}, u32[]{:S(2)}) async-start(bf16[16,64,1024]{2,1,0:T(8,128)(2,1)} %bitcast.66), calls=%async_computation.1 | async-start | bytes 4194304 | tf_op jit(solution)/shard_map/all_to_all | solution.py:118
  59.8 0.5 broadcast.219
  60.3 0.7 reduce.7
  61.1 46.0 %all-to-all-done.1 = bf16[16,64,1024]{2,1,0:T(8,128)(2,1)} async-done(((bf16[16,64,1024]{2,1,0:T(8,128)(2,1)}), bf16[16,64,1024]{2,1,0:T(8,128)(2,1)}, u32[]{:S(2)}, u32[]{:S(2)}) %all-to-all-start.1) | async-done | bytes 2097184 | tf_op jit(solution)/shard_map/all_to_all | solution.py:118
  107.0 2.1 %multiply_reduce_fusion = (f32[128]{0:T(128)S(1)}, f32[128,1024]{1,0:T(8,128)S(1)}) fusion(bf16[1024,1024]{1,0:T(8,128)(2,1)} %bitcast.9, s32[1024]{0:T(1024)S(1)} %eq.80), kind=kOutput, calls=%fused_computation.25 | convolution fusion | flops 268828544 | bytes 2626048 | tf_op jit(solution)/shard_map/dot_general | solution.py:93
  109.2 3.8 %convolution_convert_fusion = bf16[128,3072]{1,0:T(8,128)(2,1)S(1)} fusion(bf16[1024,3072]{1,0:T(8,128)(2,1)} %param.19, f32[128,1024]{1,0:T(8,128)S(1)} %get-tuple-element.11, f32[128]{0:T(128)S(1)} %add_rsqrt_fusion), kind=kOutput, calls=%fused_computation.7 | convolution fusion | flops 805961728 | bytes 7602688 | tf_op jit(solution)/shard_map/dot_general | solution.py:128
  113.0 0.8 fusion.37
  113.8 9.3 %all_gather.7 = bf16[4,64,1024]{2,1,0:T(8,128)(2,1)S(1)} all-gather(bf16[4,32,1024]{2,1,0:T(8,128)(2,1)S(1)} %bitcast.70), channel_id=1, replica_groups=mesh['cam'=16,'frame'=2] {'frame'}, dimensions={1}, use_global_device_ids=true | all-gather | bytes 786432 | tf_op jit(solution)/shard_map/all_gather | solution.py:134
  123.0 1.7 %reshape.182 = bf16[4,64,16,64]{3,2,1,0:T(8,128)(2,1)} reshape(bf16[4,64,1024]{2,1,0:T(8,128)(2,1)S(1)} %all_gather.7) | data formatting | bytes 1048576 | tf_op jit(solution)/shard_map/reshape | solution.py:152
  124.7 8.6 %all_gather.6 = bf16[4,64,1024]{2,1,0:T(8,128)(2,1)S(1)} all-gather(bf16[4,32,1024]{2,1,0:T(8,128)(2,1)} %bitcast.69), channel_id=1, replica_groups=mesh['cam'=16,'frame'=2] {'frame'}, dimensions={1}, use_global_device_ids=true | all-gather | bytes 786432 | tf_op jit(solution)/shard_map/all_gather | solution.py:133
  133.3 1.7 %reshape.180 = bf16[4,64,16,64]{3,2,1,0:T(8,128)(2,1)} reshape(bf16[4,64,1024]{2,1,0:T(8,128)(2,1)S(1)} %all_gather.6) | data formatting | bytes 1048576 | tf_op jit(solution)/shard_map/reshape | solution.py:140
  135.0 0.3 reshape.178
  135.3 2.0 %fusion.38 = (f32[4,16,32]{2,1,0:T(8,128)S(1)}, f32[4,16,32,64]{3,2,1,0:T(8,128)S(1)}) fusion(f32[4,16,64]{2,1,0:T(8,128)S(1)} %copy-done.4, bf16[4,64,16,64]{3,2,1,0:T(8,128)(2,1)} %reshape.180, bf16[4,32,16,64]{3,2,1,0:T(8,128)(2,1)S(1)} %reshape.178), kind=kOutput, calls=%fused_computation.88 | convolution fusion | flops 17168384 | bytes 1335296 | tf_op jit(solution)/shard_map/sqhd,skhd->shqk/dot_general | solution.py:137
  137.3 0.6 fusion.8
  138.0 1.9 %fusion.4 = bf16[4,32,16,64]{3,1,2,0:T(8,128)(2,1)S(1)} fusion(bf16[4,64,16,64]{3,2,1,0:T(8,128)(2,1)} %reshape.182, f32[4,16,32,64]{3,2,1,0:T(8,128)S(1)} %get-tuple-element.13, f32[4,32,16]{1,2,0:T(8,128)S(1)} %bitcast.73, f32[4,16,32]{2,1,0:T(8,128)S(1)} %broadcast_maximum_fusion.1), kind=kOutput, calls=%fused_computation.13 | convolution fusion | flops 17301504 | bytes 1327104 | tf_op jit(solution)/shard_map/shqk,skhd->shqd/dot_general | solution.py:149
  140.0 0.3 convert_element_type.51
  140.4 1.2 fusion.5
  (42 shorter events, 1.5 us)
Async XLA Ops:
  0.0 140.4 %copy-start = (bf16[1024,1024]{1,0:T(8,128)(2,1)S(1)}, bf16[1024,1024]{1,0:T(8,128)(2,1)}, u32[]{:S(2)}) copy-start(bf16[1024,1024]{1,0:T(8,128)(2,1)} %param.20) | copy-start | bytes 6291460
  0.0 19.9 %copy-start.1 = (bf16[1,32,3,4096]{3,1,2,0:T(8,128)(2,1)S(1)}, bf16[1,32,3,4096]{3,1,2,0:T(8,128)(2,1)}, u32[]{:S(2)}) copy-start(bf16[1,32,3,4096]{3,1,2,0:T(8,128)(2,1)} %param.11) | copy-start | bytes 2359300
  6.1 18.6 %copy-start.5 = (bf16[27,128]{1,0:T(8,128)(2,1)S(1)}, bf16[27,128]{1,0:T(8,128)(2,1)}, u32[]{:S(2)}) copy-start(bf16[27,128]{1,0:T(8,128)(2,1)} %param.12) | copy-start | bytes 20740
  6.1 18.6 %copy-start.7 = (bf16[1152,256]{1,0:T(8,128)(2,1)S(1)}, bf16[1152,256]{1,0:T(8,128)(2,1)}, u32[]{:S(2)}) copy-start(bf16[1152,256]{1,0:T(8,128)(2,1)} %param.13) | copy-start | bytes 1769476
  13.6 40.1 %all-to-all-start = ((s32[16,1,64]{2,1,0:T(1,128)}), s32[16,1,64]{2,1,0:T(1,128)S(1)}, u32[]{:S(2)}, u32[]{:S(2)}) async-start(s32[16,1,64]{2,1,0:T(1,128)} %all_to_all.9), calls=%async_computation | async-start | bytes 16384 | tf_op jit(solution)/shard_map/all_to_all | solution.py:119
  40.0 4.8 %copy-start.3 = (s32[1,32,12,8]{1,3,2,0:T(8,128)S(1)}, s32[1,32,12,8]{1,3,2,0:T(8,128)}, u32[]{:S(2)}) copy-start(s32[1,32,12,8]{1,3,2,0:T(8,128)} %param.17) | copy-start | bytes 36868
  40.0 4.8 %copy-start.6 = (s32[1,32,12]{1,0,2:T(1,128)S(1)}, s32[1,32,12]{1,0,2:T(1,128)}, u32[]{:S(2)}) copy-start(s32[1,32,12]{1,0,2:T(1,128)} %param.16) | copy-start | bytes 4612
  40.0 5.1 %copy-start.2 = (bf16[256,128]{1,0:T(8,128)(2,1)S(1)}, bf16[256,128]{1,0:T(8,128)(2,1)}, u32[]{:S(2)}) copy-start(bf16[256,128]{1,0:T(8,128)(2,1)} %param.14) | copy-start | bytes 196612
  53.8 53.3 %all-to-all-start.1 = ((bf16[16,64,1024]{2,1,0:T(8,128)(2,1)}), bf16[16,64,1024]{2,1,0:T(8,128)(2,1)}, u32[]{:S(2)}, u32[]{:S(2)}) async-start(bf16[16,64,1024]{2,1,0:T(8,128)(2,1)} %bitcast.66), calls=%async_computation.1 | async-start | bytes 4194304 | tf_op jit(solution)/shard_map/all_to_all | solution.py:118
  113.0 22.3 %copy-start.4 = (f32[4,16,64]{2,1,0:T(8,128)S(1)}, f32[4,16,64]{2,1,0:T(8,128)}, u32[]{:S(2)}) copy-start(f32[4,16,64]{2,1,0:T(8,128)} %param.21) | copy-start | bytes 49156
where the time goes:
time: 142 us
  waiting for transfers between devices  46 us (32%)
  local copies, waits for them, and re-layouts  30.4 us (21%)
  matrix products  27.1 us (19%)
  blocking collectives  17.9 us (13%)
  starting transfers between devices  12.3 us (9%)
  other arithmetic  7.7 us (5%)
    all_to_all x1, waiting for transfers between devices, per_device(): lax.all_to_all(outgoing, 'cam', split_axis=0, concat_axis=0, tiled=True)  46 us
    conv_general_dilated x1, matrix products, conv_features(): lax.conv_general_dilated(section_one, conv2_w.reshape(3, 3, C1, C2), (2,...  15.4 us
    all_gather x1, blocking collectives, per_device(): value_piece = lax.all_gather(value_rows, 'frame', axis=1, tiled=True)  9.25 us
    all_gather x1, blocking collectives, per_device(): key_piece = lax.all_gather(key_rows, 'frame', axis=1, tiled=True)  8.6 us
    gather x1, local copies, waits for them, and re-layouts, build_buffers(): return (outgoing, codes[source].reshape(owners, capacity))  6.87 us
    all_to_all x1, starting transfers between devices, per_device(): lax.all_to_all(codes, 'cam', split_axis=0, concat_axis=0, tiled=True)  6.24 us
    all_to_all x1, starting transfers between devices, per_device(): lax.all_to_all(outgoing, 'cam', split_axis=0, concat_axis=0, tiled=True)  6.01 us
    gather x1, local copies, waits for them, and re-layouts, build_buffers(): outgoing = padded[source].reshape(owners, capacity, payload.shape[1])  5.39 us
  transfers between devices with their start and end apart: 2, of which 1 were waited for; matrix products, arithmetic and copies ran while one was open for 25% of the time, Pallas kernels for 0%

commit v1 on v0

--- a/solution.py
+++ b/solution.py
@@ -130,8 +130,13 @@
     key_rows = mixed[:, width : 2 * width].reshape(SUBJ_DEV, frames_here, width)
     value_rows = mixed[:, 2 * width :].reshape(SUBJ_DEV, frames_here, width)
     row_top = jnp.full((SUBJ_DEV, HEADS, frames_here), NEG_START, jnp.float32)
-    key_piece = lax.all_gather(key_rows, "frame", axis=1, tiled=True)
-    value_piece = lax.all_gather(value_rows, "frame", axis=1, tiled=True)
+    key_piece, value_piece = jnp.split(
+        lax.all_gather(
+            jnp.concatenate([key_rows, value_rows], axis=0), "frame", axis=1, tiled=True
+        ),
+        [key_rows.shape[0]],
+        axis=0,
+    )
     span = key_piece.shape[1]
     scores = (
         jnp.einsum(

time: 142 us -> 164 us (1.15); the launches traced: 142 us -> 161 us
  waiting for transfers between devices: 46 us -> 66.2 us
  blocking collectives: 17.9 us -> 0 us
  between operations: 0.27 us -> 13.7 us
  local copies, waits for them, and re-layouts: 30.4 us -> 33.4 us
    all_gather x0 -> x1, waiting for transfers between devices: none -> 20.3 us  [per_device(): lax.all_gather(jnp.concatenate([key_rows, value_rows], axis=0), 'frame',...]
    all_gather x2 -> x0, blocking collectives: 17.9 us -> none  [the longest x1 9.25 us: per_device(): value_piece = lax.all_gather(value_rows, 'frame', axis=1, tiled=True)]
    split x0 -> x1, local copies, waits for them, and re-layouts: none -> 2.11 us  [per_device(): jnp.split(lax.all_gather(jnp.concatenate([key_rows, value_rows], axis=0),...]
  transfers between devices with their start and end apart: 2 -> 3, of which waited for: 1 -> 2; matrix products, arithmetic and copies ran while one was open for 25% -> 22% of each run, Pallas kernels for 0% -> 0%
where the time goes in v1:
time: 164 us; the launch traced here: 161 us
  waiting for transfers between devices  66.2 us (40%)
  local copies, waits for them, and re-layouts  33.4 us (20%)
  matrix products  27.3 us (17%)
  between operations  13.7 us (8%)
  starting transfers between devices  12.3 us (8%)
  other arithmetic  8.56 us (5%)
    all_to_all x1, waiting for transfers between devices, per_device(): lax.all_to_all(outgoing, 'cam', split_axis=0, concat_axis=0, tiled=True)  45.9 us
    all_gather x1, waiting for transfers between devices, per_device(): lax.all_gather(jnp.concatenate([key_rows, value_rows], axis=0), 'frame',...  20.3 us
    conv_general_dilated x1, matrix products, conv_features(): lax.conv_general_dilated(section_one, conv2_w.reshape(3, 3, C1, C2), (2,...  15.4 us
    gather x1, local copies, waits for them, and re-layouts, build_buffers(): return (outgoing, codes[source].reshape(owners, capacity))  6.87 us
    all_to_all x1, starting transfers between devices, per_device(): lax.all_to_all(codes, 'cam', split_axis=0, concat_axis=0, tiled=True)  6.24 us
    all_to_all x1, starting transfers between devices, per_device(): lax.all_to_all(outgoing, 'cam', split_axis=0, concat_axis=0, tiled=True)  6.01 us
    gather x1, local copies, waits for them, and re-layouts, build_buffers(): outgoing = padded[source].reshape(owners, capacity, payload.shape[1])  5.39 us
    another operation x1, local copies, waits for them, and re-layouts, conv_features(): images = pictures.reshape(amount, 3, IMG, IMG)  4.73 us
  transfers between devices with their start and end apart: 3, of which 2 were waited for; matrix products, arithmetic and copies ran while one was open for 22% of the time, Pallas kernels for 0%

profile of v1, /device:TPU:12, one launch (start us, length us, event | category | flops | bytes accessed | tf_op | source)
XLA Modules:
  0.0 161.4 jit_solution(3704364664102150055)
XLA Ops:
  6.5 0.9 copy.44
  7.6 0.8 select_reduce_fusion
  8.4 0.9 reduce-window.6
  9.6 2.9 %scatter_custom_fusion = s32[1024]{0:T(1024)S(1)} fusion(s32[384]{0:T(512)S(1)} %fusion.35, s32[384]{0:T(512)S(1)} %iota.33, s32[]{:T(128)} %constant.64.clone.1), kind=kCustom, calls=%fused_computation.79 | custom fusion | bytes 4100 | tf_op jit(solution)/shard_map/scatter | solution.py:78
  12.6 6.9 %gather_fusion = s32[1024]{0:T(1024)S(1)} fusion(s32[385]{0:T(512)S(1)} %pad_add_fusion, s32[1024]{0:T(1024)S(1)} %fusion.23), kind=kCustom, calls=%fused_computation | custom fusion | bytes 12288 | tf_op jit(solution)/shard_map/gather | solution.py:85
  19.5 0.7 all_to_all.9
  20.2 6.2 %all-to-all-start = ((s32[16,1,64]{2,1,0:T(1,128)}), s32[16,1,64]{2,1,0:T(1,128)S(1)}, u32[]{:S(2)}, u32[]{:S(2)}) async-start(s32[16,1,64]{2,1,0:T(1,128)} %all_to_all.9), calls=%async_computation | async-start | bytes 16384 | tf_op jit(solution)/shard_map/all_to_all | solution.py:119
  26.4 4.7 %copy.54 = bf16[1,32,3,4096]{1,2,3,0:T(4,128)(2,1)} copy(bf16[1,32,3,4096]{3,1,2,0:T(8,128)(2,1)S(1)} %copy-done.1) | data formatting | bytes 1572864 | tf_op jit(solution)/shard_map/reshape;squeeze | solution.py:21
  31.2 15.4 %broadcast_maximum_fusion = f32[32,16,16,256]{3,0,2,1:T(8,128)} fusion(bf16[3,3,128,256]{3,2,1,0:T(8,128)(2,1)S(1)} %bitcast.76, bf16[32,3,64,64]{0,1,3,2:T(4,128)(2,1)} %bitcast.68, bf16[3,3,3,128]{3,2,1,0:T(4,128)(2,1)S(1)} %reshape.171), kind=kOutput, calls=%fused_computation.6 | convolution fusion | flops 4864892928 | bytes 9771776 | tf_op jit(solution)/shard_map/conv_general_dilated | solution.py:31
  46.6 4.4 %reduce_sum.56 = f32[32,4,4,256]{3,0,2,1:T(8,128)S(1)} reduce(f32[32,4,4,4,4,256]{5,0,4,3,2,1:T(8,128)} %bitcast.67, f32[]{:T(128)} %constant.69.clone.1), dimensions={2,4}, to_apply=%region_5.6 | reduce | flops 1966080 | bytes 8912900 | tf_op jit(solution)/shard_map/reduce_sum | solution.py:41
  51.7 0.2 convolution_convert_fusion.2
  51.9 0.6 convolution_convert_fusion.1
  52.5 1.2 reshape.175
  53.7 1.2 concatenate.10
  54.9 5.4 %gather_fusion.1 = bf16[1024,1024]{1,0:T(8,128)(2,1)} fusion(bf16[385,1024]{1,0:T(8,128)(2,1)S(1)} %concatenate.10, s32[1024]{0:T(1024)S(1)} %fusion.23), kind=kCustom, calls=%fused_computation.1 | custom fusion | bytes 4198400 | tf_op jit(solution)/shard_map/gather | solution.py:84
  60.3 6.0 %all-to-all-start.1 = ((bf16[16,64,1024]{2,1,0:T(8,128)(2,1)}), bf16[16,64,1024]{2,1,0:T(8,128)(2,1)}, u32[]{:S(2)}, u32[]{:S(2)}) async-start(bf16[16,64,1024]{2,1,0:T(8,128)(2,1)} %bitcast.66), calls=%async_computation.1 | async-start | bytes 4194304 | tf_op jit(solution)/shard_map/all_to_all | solution.py:118
  66.4 0.5 broadcast.219
  66.9 0.7 reduce.7
  67.6 45.9 %all-to-all-done.1 = bf16[16,64,1024]{2,1,0:T(8,128)(2,1)} async-done(((bf16[16,64,1024]{2,1,0:T(8,128)(2,1)}), bf16[16,64,1024]{2,1,0:T(8,128)(2,1)}, u32[]{:S(2)}, u32[]{:S(2)}) %all-to-all-start.1) | async-done | bytes 2097184 | tf_op jit(solution)/shard_map/all_to_all | solution.py:118
  113.6 2.1 %multiply_reduce_fusion = (f32[128]{0:T(128)S(1)}, f32[128,1024]{1,0:T(8,128)S(1)}) fusion(bf16[1024,1024]{1,0:T(8,128)(2,1)} %bitcast.9, s32[1024]{0:T(1024)S(1)} %eq.80), kind=kOutput, calls=%fused_computation.26 | convolution fusion | flops 268828544 | bytes 2626048 | tf_op jit(solution)/shard_map/dot_general | solution.py:93
  115.7 3.8 %convolution_convert_fusion = bf16[128,3072]{1,0:T(8,128)(2,1)S(1)} fusion(bf16[1024,3072]{1,0:T(8,128)(2,1)} %param.19, f32[128,1024]{1,0:T(8,128)S(1)} %get-tuple-element.13, f32[128]{0:T(128)S(1)} %add_rsqrt_fusion), kind=kOutput, calls=%fused_computation.7 | convolution fusion | flops 805961728 | bytes 7602688 | tf_op jit(solution)/shard_map/dot_general | solution.py:128
  119.6 0.9 pad_maximum_fusion
  120.5 1.1 reshape.178
  121.6 20.3 %all-gather.2.cloned.1.call-done = bf16[8,64,1024]{2,1,0:T(8,128)(2,1)} async-done(((bf16[8,32,1024]{2,1,0:T(8,128)(2,1)}), bf16[8,64,1024]{2,1,0:T(8,128)(2,1)}) %all-gather.2.cloned.1.call-update) | async-done | bytes 1048592 | tf_op jit(solution)/shard_map/all_gather | solution.py:134
  141.9 2.1 %fusion.37 = (bf16[4,64,1024]{2,1,0:T(8,128)(2,1)S(1)}, bf16[4,64,1024]{2,1,0:T(8,128)(2,1)}) fusion(bf16[8,64,1024]{2,1,0:T(8,128)(2,1)} %all-gather.2.cloned.1.call-done), kind=kLoop, calls=%fused_computation.88 | loop fusion | bytes 2097152 | tf_op jit(solution)/shard_map/split | solution.py:133
  144.0 2.5 %reshape.182 = bf16[4,64,16,64]{3,2,1,0:T(8,128)(2,1)} reshape(bf16[4,64,1024]{2,1,0:T(8,128)(2,1)} %get-tuple-element.6) | data formatting | bytes 1048576 | tf_op jit(solution)/shard_map/reshape | solution.py:157
  146.5 1.7 %reshape.181 = bf16[4,64,16,64]{3,2,1,0:T(8,128)(2,1)} reshape(bf16[4,64,1024]{2,1,0:T(8,128)(2,1)S(1)} %get-tuple-element.5) | data formatting | bytes 1048576 | tf_op jit(solution)/shard_map/reshape | solution.py:145
  148.2 2.1 %fusion.39 = (f32[4,16,32]{2,1,0:T(8,128)S(1)}, f32[4,16,32,64]{3,2,1,0:T(8,128)S(1)}) fusion(f32[4,16,64]{2,1,0:T(8,128)S(1)} %copy-done.4, bf16[4,64,16,64]{3,2,1,0:T(8,128)(2,1)} %reshape.181, bf16[4,32,16,64]{3,2,1,0:T(8,128)(2,1)} %reshape.178), kind=kOutput, calls=%fused_computation.90 | convolution fusion | flops 17168384 | bytes 1335296 | tf_op jit(solution)/shard_map/sqhd,skhd->shqk/dot_general | solution.py:142
  150.3 0.6 fusion.8
  151.0 1.9 %fusion.4 = bf16[4,32,16,64]{3,1,2,0:T(8,128)(2,1)S(1)} fusion(bf16[4,64,16,64]{3,2,1,0:T(8,128)(2,1)} %reshape.182, f32[4,16,32,64]{3,2,1,0:T(8,128)S(1)} %get-tuple-element.15, f32[4,32,16]{1,2,0:T(8,128)S(1)} %bitcast.73, f32[4,16,32]{2,1,0:T(8,128)S(1)} %broadcast_maximum_fusion.1), kind=kOutput, calls=%fused_computation.13 | convolution fusion | flops 17301504 | bytes 1327104 | tf_op jit(solution)/shard_map/shqk,skhd->shqd/dot_general | solution.py:154
  153.1 0.3 convert_element_type.51
  153.4 1.2 fusion.5
  (45 shorter events, 1.6 us)
Async XLA Ops:
  6.5 146.9 %copy-start = (bf16[1024,1024]{1,0:T(8,128)(2,1)S(1)}, bf16[1024,1024]{1,0:T(8,128)(2,1)}, u32[]{:S(2)}) copy-start(bf16[1024,1024]{1,0:T(8,128)(2,1)} %param.20) | copy-start | bytes 6291460
  6.5 19.9 %copy-start.1 = (bf16[1,32,3,4096]{3,1,2,0:T(8,128)(2,1)S(1)}, bf16[1,32,3,4096]{3,1,2,0:T(8,128)(2,1)}, u32[]{:S(2)}) copy-start(bf16[1,32,3,4096]{3,1,2,0:T(8,128)(2,1)} %param.11) | copy-start | bytes 2359300
  12.6 18.6 %copy-start.5 = (bf16[27,128]{1,0:T(8,128)(2,1)S(1)}, bf16[27,128]{1,0:T(8,128)(2,1)}, u32[]{:S(2)}) copy-start(bf16[27,128]{1,0:T(8,128)(2,1)} %param.12) | copy-start | bytes 20740
  12.6 18.6 %copy-start.7 = (bf16[1152,256]{1,0:T(8,128)(2,1)S(1)}, bf16[1152,256]{1,0:T(8,128)(2,1)}, u32[]{:S(2)}) copy-start(bf16[1152,256]{1,0:T(8,128)(2,1)} %param.13) | copy-start | bytes 1769476
  20.2 40.1 %all-to-all-start = ((s32[16,1,64]{2,1,0:T(1,128)}), s32[16,1,64]{2,1,0:T(1,128)S(1)}, u32[]{:S(2)}, u32[]{:S(2)}) async-start(s32[16,1,64]{2,1,0:T(1,128)} %all_to_all.9), calls=%async_computation | async-start | bytes 16384 | tf_op jit(solution)/shard_map/all_to_all | solution.py:119
  46.6 4.8 %copy-start.3 = (s32[1,32,12,8]{1,3,2,0:T(8,128)S(1)}, s32[1,32,12,8]{1,3,2,0:T(8,128)}, u32[]{:S(2)}) copy-start(s32[1,32,12,8]{1,3,2,0:T(8,128)} %param.17) | copy-start | bytes 36868
  46.6 4.8 %copy-start.6 = (s32[1,32,12]{1,0,2:T(1,128)S(1)}, s32[1,32,12]{1,0,2:T(1,128)}, u32[]{:S(2)}) copy-start(s32[1,32,12]{1,0,2:T(1,128)} %param.16) | copy-start | bytes 4612
  46.6 5.1 %copy-start.2 = (bf16[256,128]{1,0:T(8,128)(2,1)S(1)}, bf16[256,128]{1,0:T(8,128)(2,1)}, u32[]{:S(2)}) copy-start(bf16[256,128]{1,0:T(8,128)(2,1)} %param.14) | copy-start | bytes 196612
  60.3 53.3 %all-to-all-start.1 = ((bf16[16,64,1024]{2,1,0:T(8,128)(2,1)}), bf16[16,64,1024]{2,1,0:T(8,128)(2,1)}, u32[]{:S(2)}, u32[]{:S(2)}) async-start(bf16[16,64,1024]{2,1,0:T(8,128)(2,1)} %bitcast.66), calls=%async_computation.1 | async-start | bytes 4194304 | tf_op jit(solution)/shard_map/all_to_all | solution.py:118
  66.3 75.6 %all-gather.2.cloned.1.call-start = ((), (), s32[]{:S(2)}) async-start(), calls=%async_computation.2 | async-start | bytes 1572864 | tf_op jit(solution)/shard_map/all_gather | solution.py:134
  119.6 28.6 %copy-start.4 = (f32[4,16,64]{2,1,0:T(8,128)S(1)}, f32[4,16,64]{2,1,0:T(8,128)}, u32[]{:S(2)}) copy-start(f32[4,16,64]{2,1,0:T(8,128)} %param.21) | copy-start | bytes 49156
Sparse Core Ops, SparseCore 0:
  120.6 21.2 all-gather.1
